TPU v7x, 32 devices: a whole 2x2x4 slice. The times are simulated.
32 devices in a mesh: dp: 8 (over z, y), mp: 4 (over x, core).
Axes of the slice: x: 2, y: 2, z: 4, core: 2. Of those that a mesh axis runs over, the one named last changes fastest.
Arguments:
- tokens: bfloat16 [16560, 1024], P('dp'), may hold values from -6 to 6
- offsets: int32 [48, 5], P('dp'), may hold values from 0 to 308, as said below
- first_gain: float32 [1024], replicated, may hold values from 0.1 to 1.9
- first_shift: float32 [1024], replicated, may hold values from -1.8 to 1.8
- qkv_weight: float32 [1024, 3, 1024], P('dp', None, 'mp'), may hold values from -0.1875 to 0.1875
- qv_bias: float32 [2, 1024], P(None, 'mp'), may hold values from -1.8 to 1.8
- proj_weight: float32 [1024, 1024], P('mp', 'dp'), may hold values from -0.5 to 0.5
- proj_bias: float32 [1024], replicated, may hold values from -1.8 to 1.8
- second_gain: float32 [1024], replicated, may hold values from 0.1 to 1.9
- second_shift: float32 [1024], replicated, may hold values from -1.8 to 1.8
- expand_weight: float32 [1024, 4096], P('dp', 'mp'), may hold values from -0.1875 to 0.1875
- expand_bias: float32 [4096], P('mp'), may hold values from -1.8 to 1.8
- shrink_weight: float32 [4096, 1024], P('mp', 'dp'), may hold values from -0.09375 to 0.09375
- shrink_bias: float32 [1024], replicated, may hold values from -1.8 to 1.8
- cotangent: bfloat16 [16560, 1024], P('dp'), may hold values from -6 to 6
Outputs:
- out: bfloat16 [16560, 1024], P('dp')
- d_tokens: float32 [16560, 1024], P('dp')
- d_first_gain: float32 [1024], replicated
- d_first_shift: float32 [1024], replicated
- d_qkv_weight: float32 [1024, 3, 1024], P('dp', None, 'mp')
- d_qv_bias: float32 [2, 1024], P(None, 'mp')
- d_proj_weight: float32 [1024, 1024], P('mp', 'dp')
- d_proj_bias: float32 [1024], replicated
- d_second_gain: float32 [1024], replicated
- d_second_shift: float32 [1024], replicated
- d_expand_weight: float32 [1024, 4096], P('dp', 'mp')
- d_expand_bias: float32 [4096], P('mp')
- d_shrink_weight: float32 [4096, 1024], P('mp', 'dp')
- d_shrink_bias: float32 [1024], replicated
Inputs may be any that keep to these rules, and one draw needn't show every extreme that they name: `offsets`: each row lists, rising, where the 5 crops of one crop set start within its 345 tokens: the first starts at 0, one crop spans 197 tokens, the others 37 each, and the last ends at the set's end.
All inputs are finite; a program needn't handle non-finite values.
Results may differ from a plain program's by a relative error of at most 0.015.
Values may be sent and summed in bfloat16 or wider, within the bound.
No kernel may reach another device: no remote copies, remote signals or barrier semaphores. Data moves between devices by JAX's collectives and lax.ppermute only.
A program may use at most 128 MiB of HBM per device.

v0:
```python
import jax
import jax.numpy as jnp
from jax import lax
from jax.sharding import PartitionSpec as P

HEAD_DIM = 64
SET_TOKENS = 345
norm_eps = 1e-06
masked_score = -1e30
root_half = 0.7071067811865476


def layer_norm(values, gain, shift):
    centre = jnp.mean(values, axis=-1, keepdims=True)
    offset_rows = values - centre
    spread = jnp.mean(offset_rows * offset_rows, axis=-1, keepdims=True)
    return offset_rows * lax.rsqrt(spread + norm_eps) * gain + shift


def normalized(values):
    centre = jnp.mean(values, axis=-1, keepdims=True)
    offset_rows = values - centre
    spread = jnp.mean(offset_rows * offset_rows, axis=-1, keepdims=True)
    return offset_rows * lax.rsqrt(spread + norm_eps)


def gelu(values):
    return 0.5 * values * (1.0 + lax.erf(values * root_half))


def matmul(left, right):
    return jnp.dot(left, right, preferred_element_type=jnp.float32)


def set_scores(query_rows, key_rows, crop_ids, factor):
    scores = (
        jnp.einsum("qhe,khe->hqk", query_rows, key_rows, preferred_element_type=jnp.float32)
        * factor
    )
    same_crop = crop_ids[:, None] == crop_ids[None, :]
    return jnp.where(same_crop[None], scores, masked_score)


def attend_forward(factor):

    def attend(pieces):
        query_rows, key_rows, value_rows, crop_ids = pieces
        scores = set_scores(query_rows, key_rows, crop_ids, factor)
        peak_score = jnp.max(scores, axis=-1, keepdims=True)
        raised = jnp.exp(scores - peak_score)
        row_total = jnp.sum(raised, axis=-1, keepdims=True)
        weights = (raised / row_total).astype(jnp.bfloat16)
        mixed = jnp.einsum("hqk,khe->qhe", weights, value_rows, preferred_element_type=jnp.float32)
        return (mixed.astype(jnp.bfloat16), (peak_score + jnp.log(row_total))[..., 0])

    return attend


def attend_backward(factor):

    def backward(pieces):
        query_rows, key_rows, value_rows, crop_ids, log_total, grad_mixed = pieces
        scores = set_scores(query_rows, key_rows, crop_ids, factor)
        weights = jnp.exp(scores - log_total[..., None])
        grad_values = jnp.einsum(
            "hqk,qhe->khe",
            weights.astype(jnp.bfloat16),
            grad_mixed,
            preferred_element_type=jnp.float32,
        )
        grad_weights = jnp.einsum(
            "qhe,khe->hqk", grad_mixed, value_rows, preferred_element_type=jnp.float32
        )
        grad_scores = weights * (
            grad_weights - jnp.sum(weights * grad_weights, axis=-1, keepdims=True)
        )
        scores_low = grad_scores.astype(jnp.bfloat16)
        grad_queries = (
            jnp.einsum("hqk,khe->qhe", scores_low, key_rows, preferred_element_type=jnp.float32)
            * factor
        )
        grad_keys = (
            jnp.einsum("hqk,qhe->khe", scores_low, query_rows, preferred_element_type=jnp.float32)
            * factor
        )
        return (grad_queries, grad_keys, grad_values)

    return backward


def shards(
    tokens,
    offsets,
    first_gain,
    first_shift,
    qkv_weight,
    qv_bias,
    proj_weight,
    proj_bias,
    second_gain,
    second_shift,
    expand_weight,
    expand_bias,
    shrink_weight,
    shrink_bias,
    cotangent,
):
    row_count = tokens.shape[0]
    sets_here = offsets.shape[0]
    width_here = qkv_weight.shape[2]
    local_heads = width_here // HEAD_DIM
    factor = HEAD_DIM ** (-0.5)
    model_count = lax.axis_size("mp")
    model_index = lax.axis_index("mp")
    extra = -row_count % model_count
    share_rows = (row_count + extra) // model_count
    share_start = model_index * share_rows
    row_numbers = jnp.arange(row_count, dtype=jnp.int32)
    row_mask = ((row_numbers >= share_start) & (row_numbers < share_start + share_rows)).astype(
        jnp.float32
    )[:, None]
    positions = jnp.arange(SET_TOKENS, dtype=jnp.int32)
    crop_ids = jnp.sum((positions[None, :, None] >= offsets[:, None, :]).astype(jnp.int32), axis=-1)
    qkv_master = qkv_weight.astype(jnp.bfloat16)
    proj_master = proj_weight.astype(jnp.bfloat16)
    expand_master = expand_weight.astype(jnp.bfloat16)
    shrink_master = shrink_weight.astype(jnp.bfloat16)
    qkv_full, proj_full, expand_full, shrink_full = (
        lax.all_gather(qkv_master, "dp", axis=0, tiled=True),
        lax.all_gather(proj_master, "dp", axis=1, tiled=True),
        lax.all_gather(expand_master, "dp", axis=0, tiled=True),
        lax.all_gather(shrink_master, "dp", axis=1, tiled=True),
    )
    inputs = tokens.astype(jnp.float32)
    first_low = layer_norm(inputs, first_gain, first_shift).astype(jnp.bfloat16)
    projected = jnp.einsum("td,dcf->tcf", first_low, qkv_full, preferred_element_type=jnp.float32)
    shaped = (sets_here, SET_TOKENS, local_heads, HEAD_DIM)
    query_rows = (projected[:, 0] + qv_bias[0]).astype(jnp.bfloat16).reshape(shaped)
    key_rows = projected[:, 1].astype(jnp.bfloat16).reshape(shaped)
    value_rows = (projected[:, 2] + qv_bias[1]).astype(jnp.bfloat16).reshape(shaped)
    attended, log_total = lax.map(
        attend_forward(factor), (query_rows, key_rows, value_rows, crop_ids)
    )
    attended_flat = attended.reshape(row_count, width_here)
    attn_part = matmul(attended_flat, proj_full)
    residual = inputs + lax.psum(attn_part, "mp") + proj_bias
    second_low = layer_norm(residual, second_gain, second_shift).astype(jnp.bfloat16)
    hidden_pre = matmul(second_low, expand_full) + expand_bias
    hidden = gelu(hidden_pre).astype(jnp.bfloat16)
    mlp_part = matmul(hidden, shrink_full)
    outputs = (
        residual + lax.psum(mlp_part.astype(jnp.bfloat16), "mp").astype(jnp.float32) + shrink_bias
    ).astype(jnp.bfloat16)
    grad_out = cotangent.astype(jnp.float32)
    shrink_grad = jnp.einsum("tf,td->fd", hidden, cotangent, preferred_element_type=jnp.float32)
    grad_hidden = jnp.einsum(
        "td,fd->tf", cotangent, shrink_full, preferred_element_type=jnp.float32
    )
    _, gelu_pull = jax.vjp(gelu, hidden_pre)
    grad_pre = gelu_pull(grad_hidden)[0]
    expand_bias_grad = jnp.sum(grad_pre, axis=0)
    grad_pre_low = grad_pre.astype(jnp.bfloat16)
    expand_grad = jnp.einsum(
        "td,tf->df", second_low, grad_pre_low, preferred_element_type=jnp.float32
    )
    second_part = jnp.einsum(
        "tf,df->td", grad_pre_low, expand_full, preferred_element_type=jnp.float32
    )
    grad_second = lax.psum(second_part, "mp")
    _, second_pull = jax.vjp(lambda values: layer_norm(values, second_gain, second_shift), residual)
    grad_residual = second_pull(grad_second)[0] + grad_out
    grad_second_kept = grad_second * row_mask
    second_gain_grad = jnp.sum(grad_second_kept * normalized(residual), axis=0)
    second_shift_grad = jnp.sum(grad_second_kept, axis=0)
    proj_bias_grad = jnp.sum(grad_residual * row_mask, axis=0)
    shrink_bias_grad = jnp.sum(grad_out * row_mask, axis=0)
    residual_low = grad_residual.astype(jnp.bfloat16)
    proj_grad = jnp.einsum(
        "tc,td->cd", attended_flat, residual_low, preferred_element_type=jnp.float32
    )
    grad_attended = jnp.einsum(
        "td,cd->tc", residual_low, proj_full, preferred_element_type=jnp.float32
    ).astype(jnp.bfloat16)
    grad_queries, grad_keys, grad_values = lax.map(
        attend_backward(factor),
        (query_rows, key_rows, value_rows, crop_ids, log_total, grad_attended.reshape(shaped)),
    )
    grad_queries = grad_queries.reshape(row_count, width_here)
    grad_keys = grad_keys.reshape(row_count, width_here)
    grad_values = grad_values.reshape(row_count, width_here)
    qv_bias_grad = jnp.stack([jnp.sum(grad_queries, axis=0), jnp.sum(grad_values, axis=0)])
    grad_projected = jnp.stack([grad_queries, grad_keys, grad_values], axis=1).astype(jnp.bfloat16)
    qkv_grad = jnp.einsum(
        "td,tcf->dcf", first_low, grad_projected, preferred_element_type=jnp.float32
    )
    first_part = jnp.einsum(
        "tcf,dcf->td", grad_projected, qkv_full, preferred_element_type=jnp.float32
    )
    grad_first = lax.psum(first_part.astype(jnp.bfloat16), "mp").astype(jnp.float32)
    _, first_pull = jax.vjp(lambda values: layer_norm(values, first_gain, first_shift), inputs)
    grad_tokens = first_pull(grad_first)[0] + grad_residual
    grad_first_kept = grad_first * row_mask
    first_gain_grad = jnp.sum(grad_first_kept * normalized(inputs), axis=0)
    first_shift_grad = jnp.sum(grad_first_kept, axis=0)
    qkv_part, proj_part, expand_part, shrink_part = (
        lax.psum_scatter(
            qkv_grad.astype(jnp.bfloat16), "dp", scatter_dimension=0, tiled=True
        ).astype(jnp.float32),
        lax.psum_scatter(
            proj_grad.astype(jnp.bfloat16), "dp", scatter_dimension=1, tiled=True
        ).astype(jnp.float32),
        lax.psum_scatter(
            expand_grad.astype(jnp.bfloat16), "dp", scatter_dimension=0, tiled=True
        ).astype(jnp.float32),
        lax.psum_scatter(
            shrink_grad.astype(jnp.bfloat16), "dp", scatter_dimension=1, tiled=True
        ).astype(jnp.float32),
    )
    qv_part, expand_bias_part = lax.psum((qv_bias_grad, expand_bias_grad), "dp")
    small_parts = lax.psum(
        (
            first_gain_grad,
            first_shift_grad,
            proj_bias_grad,
            second_gain_grad,
            second_shift_grad,
            shrink_bias_grad,
        ),
        ("dp", "mp"),
    )
    return (
        outputs,
        grad_tokens,
        small_parts[0],
        small_parts[1],
        qkv_part,
        qv_part,
        proj_part,
        small_parts[2],
        small_parts[3],
        small_parts[4],
        expand_part,
        expand_bias_part,
        shrink_part,
        small_parts[5],
    )


def solution(mesh):
    placed = (
        P("dp", None),
        P("dp", None),
        P(),
        P(),
        P("dp", None, "mp"),
        P(None, "mp"),
        P("mp", "dp"),
        P(),
        P(),
        P(),
        P("dp", "mp"),
        P("mp"),
        P("mp", "dp"),
        P(),
        P("dp", None),
    )
    return jax.shard_map(
        shards,
        mesh=mesh,
        in_specs=placed,
        out_specs=(
            P("dp", None),
            P("dp", None),
            P(),
            P(),
            P("dp", None, "mp"),
            P(None, "mp"),
            P("mp", "dp"),
            P(),
            P(),
            P(),
            P("dp", "mp"),
            P("mp"),
            P("mp", "dp"),
            P(),
        ),
        check_vma=False,
    )
```

profile of v0, /device:TPU:0, one launch (start us, length us, event | category | flops | bytes accessed | tf_op | source)
XLA Modules:
  0.0 1080.6 jit_solution(10375636445222786847)
XLA Ops:
  11.9 3.0 convert_reduce_fusion
  16.9 34.5 %all_gather.13 = bf16[256,1024]{1,0:T(8,128)(2,1)} all-gather(bf16[256,128]{1,0:T(8,128)(2,1)S(1)} %convert_element_type.121), channel_id=1, replica_groups=mesh['dp'=8,'mp'=4] {'dp'}, dimensions={1}, use_global_device_ids=true | all-gather | bytes 589824 | tf_op jit(solution)/shard_map/all_gather | solution.py:130
  51.4 10.1 all-gather.4.cloned.1.call-done
  61.5 6.4 fusion.74
  72.6 3.0 squeeze.36
  76.2 4.4 reshape.221
  80.6 3.9 copy.95
  84.6 3.0 copy.89
  87.5 4.2 squeeze.35
  94.1 20.2 %while.26 = (s32[]{:T(128)}, bf16[6,345,4,64]{1,3,2,0:T(8,128)(2,1)}, f32[6,4,345]{2,1,0:T(4,128)}, bf16[6,345,4,64]{1,3,2,0:T(8,128)(2,1)S(1)}, s32[6,345]{1,0:...) while((s32[]{:T(128)}, ...), condition=%wide.region_6.7_spmd, body=%wide.region_3.6_spmd.sunk | while | flops 127800768 | bytes 7318627 | solution.py:141
  115.3 3.2 copy.96
  118.5 2.7 reshape.209
  121.2 6.1 fusion.87
  130.2 151.0 %all-reduce.7.cloned.1.call-done = f32[2070,1024]{1,0:T(8,128)} async-done(((f32[2070,1024]{1,0:T(8,128)}), f32[2070,1024]{1,0:T(8,128)}) %all-reduce.7.cloned.1.call-update) | async-done | bytes 8478736 | tf_op jit(solution)/shard_map/psum | solution.py:146
  281.3 5.8 fusion.82
  290.3 2.9 add_convert_fusion.1
  293.3 40.2 %all-gather.6.cloned.1.call-done = bf16[1024,1024]{1,0:T(8,128)(2,1)} async-done(((bf16[128,1024]{1,0:T(8,128)(2,1)}), bf16[1024,1024]{1,0:T(8,128)(2,1)}) %all-gather.6.cloned.1.call-update) | async-done | bytes 2097168 | tf_op jit(solution)/shard_map/all_gather | solution.py:131
  333.5 10.9 %fusion.88 = f32[2070,1024]{1,0:T(8,128)} fusion(bf16[2070,1024]{1,0:T(8,128)(2,1)} %add_convert_fusion.1, bf16[1024,1024]{1,0:T(8,128)(2,1)} %all-gather.6.cloned.1.call-done), kind=kOutput, calls=%fused_computation.143 | convolution fusion | flops 4341104640 | bytes 14815232 | tf_op jit(solution)/shard_map/dot_general | solution.py:32
  344.4 41.4 %all-gather.8.cloned.1.call-done = bf16[1024,1024]{1,0:T(8,128)(2,1)} async-done(((bf16[1024,128]{1,0:T(8,128)(2,1)}), bf16[1024,1024]{1,0:T(8,128)(2,1)}) %all-gather.8.cloned.1.call-update) | async-done | bytes 2097168 | tf_op jit(solution)/shard_map/all_gather | solution.py:132
  385.8 13.9 %fusion.80 = (f32[1024]{0:T(1024)}, bf16[2070,1024]{1,0:T(8,128)(2,1)S(1)}, bf16[2070,1024]{1,0:T(8,128)(2,1)}) fusion(f32[2070,1024]{1,0:T(8,128)} %fusion.88, f32[1024]{0:T(1024)S(1)} %copy-done.29, bf16[2070,1024]{1,0:T(8,128)(2,1)} %param.33, bf16[1024,1024]{1,0:T(8,128)(2,1)} %all-gather.8.cloned.1.call-done), kind=kOutput, calls=%fused_computation.136 | convolution fusion | flops 4377138176 | bytes 23302144 | tf_op jit(solution)/shard_map/td,fd->tf/dot_general | solution.py:156
  401.7 7.2 fusion.65
  408.9 9.5 convolution_convert_fusion.3
  418.4 3.9 copy.119
  422.5 9.2 fusion.67
  431.7 130.3 %all-reduce.9.cloned.1.call-done = f32[2070,1024]{1,0:T(8,128)} async-done(((f32[2070,1024]{1,0:T(8,128)}), f32[2070,1024]{1,0:T(8,128)}) %all-reduce.9.cloned.1.call-update) | async-done | bytes 8478736 | tf_op jit(solution)/shard_map/psum | solution.py:169
  562.0 8.2 multiply_reduce_fusion.1
  570.3 5.7 fusion.81
  576.0 3.4 copy-done.2
  583.3 4.0 copy.100
  587.3 46.0 %while.27 = (s32[]{:T(128)}, f32[6,345,4,64]{1,3,2,0:T(8,128)}, bf16[6,345,4,64]{1,3,2,0:T(8,128)(2,1)}, f32[6,345,4,64]{1,3,2,0:T(8,128)}, bf16[6,345,4,64]{1,3...) while((s32[]{:T(128)}, f32[6,345,4,64]{1,3,2,0:T(8,128)}, ...), condition=%wide.region_16.17_spmd, body=%wide.region_14.16_spmd.sunk | while | flops 309283200 | bytes 17905568 | solution.py:184
  633.3 7.1 fusion.70
  641.4 5.6 fusion.85
  647.0 4.0 copy.114
  656.6 3.9 copy.115
  660.6 2.5 reshape.215
  668.8 9.3 convolution_convert_fusion.4
  678.3 9.7 convolution_convert_fusion.1
  687.9 5.1 bitcast_convert_fusion
  695.0 8.4 reduce-scatter.11.cloned.1.call-done
  705.5 20.3 %all-reduce.1 = (f32[2,256]{1,0:T(2,128)}, f32[1024]{0:T(1024)}) all-reduce(f32[2,256]{1,0:T(2,128)S(1)} %pad_maximum_fusion, f32[1024]{0:T(1024)S(1)} %copy-done.25), channel_id=1, replica_groups=mesh['dp'=8,'mp'=4] {'dp'}, use_global_device_ids=true, to_apply=%region_27.28 | all-reduce | flops 1536 | bytes 12288 | tf_op jit(solution)/shard_map/psum | solution.py:219
  725.7 42.0 %reduce-scatter.13.cloned.1.call-done = bf16[128,256]{1,0:T(8,128)(2,1)} async-done(((bf16[1024,256]{1,0:T(8,128)(2,1)}), bf16[128,256]{1,0:T(8,128)(2,1)}) %reduce-scatter.13.cloned.1.call-update) | async-done | bytes 65552
  769.4 66.7 %reduce-scatter.9.cloned.1.call-done = bf16[128,3,256]{2,0,1:T(8,128)(2,1)} async-done(((bf16[1024,3,256]{2,0,1:T(8,128)(2,1)}), bf16[128,3,256]{2,0,1:T(8,128)(2,1)}) %reduce-scatter.9.cloned.1.call-update) | async-done | bytes 196624 | tf_op jit(solution)/shard_map/reduce_scatter | solution.py:206
  837.8 155.5 %all-reduce.11.cloned.1.call-done = (bf16[2070,1024]{1,0:T(8,128)(2,1)}, bf16[2070,1024]{1,0:T(8,128)(2,1)}) async-done(((bf16[2070,1024]{1,0:T(8,128)(2,1)}, bf16[2070,1024]{1,0:T(8,128)(2,1)}), (bf16[2070,1024]{1,0:T(8,128)(2,1)}, bf16[2070,1024]{1,0:T(8,128)(2,1)})) %all-reduce.11.cloned.1.call-update) | async-done | bytes 8478736 | tf_op jit(solution)/shard_map/psum | solution.py:152
  993.3 5.4 fusion.56
  998.8 13.9 %fusion.54 = (f32[1024]{0:T(1024)S(1)}, f32[1024]{0:T(1024)S(1)}, f32[1024]{0:T(1024)S(1)}, f32[2070]{0:T(1024)S(1)}, f32[1024]{0:T(1024)S(1)}) fusion(bf16[2070,1024]{1,0:T(8,128)(2,1)} %param.33, f32[2070]{0:T(1024)S(1)} %copy-done.15, f32[2070,1024]{1,0:T(8,128)} %copy-done.2, f32[2070]{0:T(1024)S(1)} %negate_multiply_fusion.1, ...), kind=kLoop, calls=%fused_computation.79 | loop fusion | flops 44507112 | bytes 21266960 | tf_op jit(solution)/shard_map/reduce_sum | solution.py:176
  1012.7 13.7 %add_add_fusion.2 = f32[2070,1024]{1,0:T(8,128)} fusion(bf16[2070,1024]{1,0:T(8,128)(2,1)} %param.19, bf16[2070,1024]{1,0:T(8,128)(2,1)} %get-tuple-element.235, f32[2070]{0:T(1024)S(1)} %negate_multiply_fusion, f32[2070]{0:T(1024)S(1)} %multiply_multiply_fusion, f32[1024]{0:T(1024)S(1)} %copy-done.21, f32[2070]{0:T(1024)S(1)} %copy-done.13, ...), kind=kLoop, calls=%fused_computation.86 | loop fusion | flops 27555840 | bytes 29721016 | tf_op jit(solution)/shard_map/add | solution.py:201
  1026.4 7.1 add_convert_fusion
  1033.5 40.0 %all-reduce = (f32[1024]{0:T(1024)}, f32[1024]{0:T(1024)}, f32[1024]{0:T(1024)}, f32[1024]{0:T(1024)}, f32[1024]{0:T(1024)}, /*index=5*/f32[1024]{0:T(1024)}) all-reduce(f32[1024]{0:T(1024)S(1)} %get-tuple-element.189, f32[1024]{0:T(1024)S(1)} %get-tuple-element.187, ...), channel_id=1, replica_groups=mesh['dp'=8,'mp'=4] {'dp','mp'}, use_global_device_ids=true, to_apply=%region_21.22 | all-reduce | flops 6144 | bytes 49152 | tf_op jit(solution)/shard_map/psum | solution.py:220
  (236 shorter events, 113.0 us)
Async XLA Ops:
  7.2 54.3 %all-gather.4.cloned.1.call-start = ((), (), s32[]{:S(2)}) async-start(), calls=%async_computation.4 | async-start | bytes 1769472 | tf_op jit(solution)/shard_map/all_gather | solution.py:129
  8.9 272.3 %all-reduce.7.cloned.1.call-start = ((), (), s32[]{:S(2)}) async-start(), calls=%async_computation.5 | async-start | bytes 16973824 | tf_op jit(solution)/shard_map/psum | solution.py:146
  10.7 4.2 copy-start.1
  11.9 49.6 %copy-start.20 = (f32[1024]{0:T(1024)S(1)}, f32[1024]{0:T(1024)}, u32[]{:S(2)}) copy-start(f32[1024]{0:T(1024)} %param.21) | copy-start | bytes 12292
  11.9 49.6 %copy-start.30 = (f32[1024]{0:T(1024)S(1)}, f32[1024]{0:T(1024)}, u32[]{:S(2)}) copy-start(f32[1024]{0:T(1024)} %param.22) | copy-start | bytes 12292
  15.0 53.0 %copy-start.10 = (f32[2070]{0:T(1024)}, f32[2070]{0:T(1024)S(1)}, u32[]{:S(2)}) copy-start(f32[2070]{0:T(1024)S(1)} %broadcast_multiply_fusion.1) | copy-start | bytes 24844
  16.3 0.6 copy-start.16
  16.9 51.1 %copy-start.12 = (f32[2070]{0:T(1024)}, f32[2070]{0:T(1024)S(1)}, u32[]{:S(2)}) copy-start(f32[2070]{0:T(1024)S(1)} %fusion.78) | copy-start | bytes 24844
  114.3 1.0 copy-start.5
  114.3 13.1 %copy-start.18 = (s32[6,345]{1,0:T(8,128)}, s32[6,345]{1,0:T(8,128)S(1)}, u32[]{:S(2)}) copy-start(s32[6,345]{1,0:T(8,128)S(1)} %get-tuple-element.473) | copy-start | bytes 24844
  121.2 6.2 copy-start.4
  127.4 1.0 copy-start.7
  127.4 1.9 copy-start.8
  127.4 153.9 %copy-start.26 = (f32[1024]{0:T(1024)S(1)}, f32[1024]{0:T(1024)}, u32[]{:S(2)}) copy-start(f32[1024]{0:T(1024)} %param.26) | copy-start | bytes 12292
  127.4 206.1 %all-gather.6.cloned.1.call-start = ((), (), s32[]{:S(2)}) async-start(), calls=%async_computation.6 | async-start | bytes 2359296 | tf_op jit(solution)/shard_map/all_gather | solution.py:131
  129.2 256.6 %all-gather.8.cloned.1.call-start = ((), (), s32[]{:S(2)}) async-start(), calls=%async_computation.7 | async-start | bytes 2359296 | tf_op jit(solution)/shard_map/all_gather | solution.py:132
  130.0 432.0 %all-reduce.9.cloned.1.call-start = ((), (), s32[]{:S(2)}) async-start(), calls=%async_computation.8 | async-start | bytes 16973824 | tf_op jit(solution)/shard_map/psum | solution.py:169
  287.1 3.3 copy-start
  287.1 3.2 copy-start.19
  287.1 3.2 copy-start.23
  293.3 92.5 %copy-start.29 = (f32[1024]{0:T(1024)S(1)}, f32[1024]{0:T(1024)}, u32[]{:S(2)}) copy-start(f32[1024]{0:T(1024)} %param.30) | copy-start | bytes 12292
  385.8 15.9 %copy-start.27 = (bf16[1024,1024]{1,0:T(8,128)(2,1)S(1)}, bf16[1024,1024]{1,0:T(8,128)(2,1)}, u32[]{:S(2)}) copy-start(bf16[1024,1024]{1,0:T(8,128)(2,1)} %all-gather.6.cloned.1.call-done) | copy-start | bytes 6291460
  399.7 2.0 copy-start.32
  408.8 284.2 %reduce-scatter.15.cloned.1.call-start = ((), (), s32[]{:S(2)}) async-start(), calls=%async_computation.12 | async-start | bytes 2359296
  422.4 281.1 %reduce-scatter.11.cloned.1.call-start = ((), (), s32[]{:S(2)}) async-start(), calls=%async_computation.10 | async-start | bytes 2359296 | tf_op jit(solution)/shard_map/reduce_scatter | solution.py:212
  422.5 139.5 %copy-start.14 = (f32[2070]{0:T(1024)}, f32[2070]{0:T(1024)S(1)}, u32[]{:S(2)}) copy-start(f32[2070]{0:T(1024)S(1)} %fusion.77) | copy-start | bytes 24844
  431.7 336.1 %reduce-scatter.13.cloned.1.call-start = ((), (), s32[]{:S(2)}) async-start(), calls=%async_computation.11 | async-start | bytes 589824
  562.0 8.3 copy-start.3
  562.0 17.4 %slice-start = ((s8[4243456]{0:T(1024)(128)(4,1)}), s8[4194304]{0:T(1024)(128)(4,1)S(1)}, s32[]{:S(2)}) async-start(s8[4243456]{0:T(1024)(128)(4,1)} %bitcast.139), calls=%async_computation.14 | async-start | bytes 8388608
  570.3 9.1 slice-start.1
  570.3 9.1 copy-start.6
  576.0 3.4 copy-start.2
  660.5 8.3 copy-start.11
  660.5 8.3 copy-start.13
  660.5 8.3 copy-start.21
  660.6 8.3 copy-start.31
  665.4 170.7 %reduce-scatter.9.cloned.1.call-start = ((), (), s32[]{:S(2)}) async-start(), calls=%async_computation.9 | async-start | bytes 1769472 | tf_op jit(solution)/shard_map/reduce_scatter | solution.py:206
  678.2 9.7 copy-start.9
  678.2 315.1 %all-reduce.11.cloned.1.call-start = ((), (), s32[]{:S(2)}) async-start(), calls=%async_computation.13 | async-start | bytes 16973824 | tf_op jit(solution)/shard_map/psum | solution.py:152
  678.2 9.7 copy-start.28
  693.0 12.4 %copy-start.25 = (f32[1024]{0:T(1024)S(1)}, f32[1024]{0:T(1024)}, u32[]{:S(2)}) copy-start(f32[1024]{0:T(1024)} %get-tuple-element.236) | copy-start | bytes 12292
  993.3 5.4 copy-start.17
  993.3 5.4 copy-start.15
  998.8 27.6 %slice-start.2 = ((s8[4243456]{0:T(1024)(128)(4,1)}), s8[49152]{0:T(1024)(128)(4,1)S(1)}, s32[]{:S(2)}) async-start(s8[4243456]{0:T(1024)(128)(4,1)} %bitcast.142), calls=%async_computation.16 | async-start | bytes 98304
  1012.7 13.7 %slice-start.3 = ((s8[4243456]{0:T(1024)(128)(4,1)}), s8[4194304]{0:T(1024)(128)(4,1)S(1)}, s32[]{:S(2)}) async-start(s8[4243456]{0:T(1024)(128)(4,1)} %bitcast.142), calls=%async_computation.17 | async-start | bytes 8388608
  1012.7 13.7 %copy-start.24 = (f32[1024]{0:T(1024)S(1)}, f32[1024]{0:T(1024)}, u32[]{:S(2)}) copy-start(f32[1024]{0:T(1024)} %param.32) | copy-start | bytes 12292
  1026.4 7.1 copy-start.22
Sparse Core Ops, SparseCore 0:
  10.8 50.6 all-gather.3
  127.6 153.6 all-reduce.6
  284.2 49.2 all-gather.5
  336.2 49.5 all-gather.7
  409.0 152.9 all-reduce.8
  565.4 67.6 reduce-scatter.14
  636.6 66.8 reduce-scatter.10
  706.8 60.8 reduce-scatter.12
  771.6 64.4 reduce-scatter.8
  839.1 154.1 all-reduce.10
where the time goes:
time: 1080 us
  waiting for transfers between devices  646 us (60%)
  matrix products  143 us (13%)
  other arithmetic  95.7 us (9%)
  blocking collectives  94.8 us (9%)
  local copies, waits for them, and re-layouts  85.2 us (8%)
  between operations  15 us (1%)
    psum x1, waiting for transfers between devices, shards(): lax.psum(mlp_part.astype(jnp.bfloat16), 'mp').astype(jnp.float32)  156 us
    psum x1, waiting for transfers between devices, shards(): residual = inputs + lax.psum(attn_part, 'mp') + proj_bias  151 us
    psum x1, waiting for transfers between devices, shards(): grad_second = lax.psum(second_part, 'mp')  130 us
    reduce_scatter x1, waiting for transfers between devices, shards(): lax.psum_scatter(qkv_grad.astype(jnp.bfloat16), 'dp', scatter_dimension=0...  66.7 us
    unnamed x12, waiting for transfers between devices  42.2 us
    all_gather x1, waiting for transfers between devices, shards(): lax.all_gather(shrink_master, 'dp', axis=1, tiled=True)  41.4 us
    all_gather x1, waiting for transfers between devices, shards(): lax.all_gather(expand_master, 'dp', axis=0, tiled=True)  40.2 us
    psum x1, blocking collectives, shards(): lax.psum((first_gain_grad, first_shift_grad, proj_bias_grad, second_gain_...  40 us
  transfers between devices with their start and end apart: 10, of which 9 were waited for; matrix products, arithmetic and copies ran while one was open for 17% of the time, Pallas kernels for 0%

commit v1 on v0

--- a/solution.py
+++ b/solution.py
@@ -8,6 +8,15 @@
 norm_eps = 1e-06
 masked_score = -1e30
 root_half = 0.7071067811865476
+
+
+def try_all_sector(my_data, k_dim):
+    my_data = jnp.moveaxis(my_data, 0, k_dim)
+    block_last = my_data.shape
+    local_now = my_data.reshape(
+        *block_last[:k_dim], block_last[k_dim] * block_last[k_dim + 1], *block_last[k_dim + 2 :]
+    )
+    return local_now
 
 
 def layer_norm(values, gain, shift):
@@ -105,6 +114,29 @@
     shrink_bias,
     cotangent,
 ):
+
+    def recast_ladders(x_local, mesh_ax, dim_at):
+        cores_n = lax.axis_size(mesh_ax)
+        items = [(dev_i, (dev_i + 1) % cores_n) for dev_i in range(cores_n)]
+        store = [(ii, jj) for jj, ii in items]
+        all_rows, arr_out = ([], [])
+        for i0 in tuple(range(cores_n - 1)):
+            if i0 % 2 == 0:
+                all_rows.append(
+                    lax.ppermute(
+                        all_rows[-1] if all_rows else x_local, axis_name=mesh_ax, perm=items
+                    )
+                )
+            else:
+                arr_out.append(
+                    lax.ppermute(arr_out[-1] if arr_out else x_local, axis_name=mesh_ax, perm=store)
+                )
+        e_next = jnp.stack([*all_rows[::-1], x_local, *arr_out], axis=0)
+        near = lax.axis_index(mesh_ax) - len(all_rows)
+        e_next = e_next[(jnp.arange(cores_n) - near) % cores_n]
+        v_now = try_all_sector(e_next, dim_at)
+        return v_now
+
     row_count = tokens.shape[0]
     sets_here = offsets.shape[0]
     width_here = qkv_weight.shape[2]
@@ -128,7 +160,7 @@
     qkv_full, proj_full, expand_full, shrink_full = (
         lax.all_gather(qkv_master, "dp", axis=0, tiled=True),
         lax.all_gather(proj_master, "dp", axis=1, tiled=True),
-        lax.all_gather(expand_master, "dp", axis=0, tiled=True),
+        recast_ladders(expand_master, "dp", 0),
         lax.all_gather(shrink_master, "dp", axis=1, tiled=True),
     )
     inputs = tokens.astype(jnp.float32)

time: 1080 us -> 990 us (0.917)
  waiting for transfers between devices: 646 us -> 527 us
  starting transfers between devices: 0.59 us -> 16 us
    psum x1, waiting for transfers between devices: 151 us -> 84.5 us  [shards(): residual = inputs + lax.psum(attn_part, 'mp') + proj_bias]
    all_gather x1, waiting for transfers between devices: 41.4 us -> 0.01 us  [shards(): lax.all_gather(shrink_master, 'dp', axis=1, tiled=True)]
    all_gather x1 -> x0, waiting for transfers between devices: 40.2 us -> none  [shards(): lax.all_gather(expand_master, 'dp', axis=0, tiled=True)]
    ppermute x0 -> x7, waiting for transfers between devices: none -> 29.5 us  [the longest x4 29.5 us: recast_ladders(): lax.ppermute(all_rows[-1] if all_rows else x_local, axis_name=mesh_ax, pe...]
    ppermute x0 -> x7, starting transfers between devices: none -> 15 us  [the longest x3 9.32 us: recast_ladders(): lax.ppermute(arr_out[-1] if arr_out else x_local, axis_name=mesh_ax, perm...]
    unnamed x81 -> x97, local copies, waits for them, and re-layouts: 22.8 us -> 28.9 us
    unnamed x12 -> x11, waiting for transfers between devices: 42.2 us -> 42.2 us
  transfers between devices with their start and end apart: 10 -> 16, of which waited for: 9 -> 11; matrix products, arithmetic and copies ran while one was open for 17% -> 26% of each run, Pallas kernels for 0% -> 0%
where the time goes in v1:
time: 990 us; the launch traced here: 985 us
  waiting for transfers between devices  527 us (53%)
  matrix products  147 us (15%)
  local copies, waits for them, and re-layouts  94.8 us (10%)
  blocking collectives  93.7 us (9%)
  other arithmetic  91.1 us (9%)
  starting transfers between devices  16 us (2%)
  between operations  14.8 us (1%)
    psum x1, waiting for transfers between devices, shards(): lax.psum(mlp_part.astype(jnp.bfloat16), 'mp').astype(jnp.float32)  156 us
    psum x1, waiting for transfers between devices, shards(): grad_second = lax.psum(second_part, 'mp')  129 us
    psum x1, waiting for transfers between devices, shards(): residual = inputs + lax.psum(attn_part, 'mp') + proj_bias  84.5 us
    reduce_scatter x1, waiting for transfers between devices, shards(): lax.psum_scatter(qkv_grad.astype(jnp.bfloat16), 'dp', scatter_dimension=0...  66.7 us
    unnamed x11, waiting for transfers between devices  42.2 us
    psum x1, blocking collectives, shards(): lax.psum((first_gain_grad, first_shift_grad, proj_bias_grad, second_gain_...  39.9 us
    all_gather x1, blocking collectives, shards(): lax.all_gather(proj_master, 'dp', axis=1, tiled=True)  33.5 us
    dot_general x3, matrix products, matmul(): return jnp.dot(left, right, preferred_element_type=jnp.float32)  30.1 us
  transfers between devices with their start and end apart: 16, of which 11 were waited for; matrix products, arithmetic and copies ran while one was open for 26% of the time, Pallas kernels for 0%

profile of v1, /device:TPU:0, one launch (start us, length us, event | category | flops | bytes accessed | tf_op | source)
XLA Modules:
  0.0 985.0 jit_solution(11312355912221909215)
XLA Ops:
  10.9 3.0 convert_reduce_fusion
  16.6 33.5 %all_gather.10 = bf16[256,1024]{1,0:T(8,128)(2,1)} all-gather(bf16[256,128]{1,0:T(8,128)(2,1)S(1)} %convert_element_type.121), channel_id=1, replica_groups=mesh['dp'=8,'mp'=4] {'dp'}, dimensions={1}, use_global_device_ids=true | all-gather | bytes 589824 | tf_op jit(solution)/shard_map/all_gather | solution.py:162
  50.2 10.6 %all-gather.3.cloned.1.call-done = bf16[1024,3,256]{2,0,1:T(8,128)(2,1)} async-done(((bf16[128,3,256]{2,0,1:T(8,128)(2,1)}), bf16[1024,3,256]{2,0,1:T(8,128)(2,1)}) %all-gather.3.cloned.1.call-update) | async-done | bytes 1572880 | tf_op jit(solution)/shard_map/all_gather | solution.py:161
  60.8 6.5 fusion.74
  71.9 3.0 squeeze.35
  76.6 3.0 copy.91
  79.5 3.0 squeeze.36
  83.2 4.6 reshape.282
  87.7 3.9 copy.95
  91.7 21.8 %while.26 = (s32[]{:T(128)}, bf16[6,345,4,64]{1,3,2,0:T(8,128)(2,1)S(1)}, f32[6,4,345]{2,1,0:T(4,128)}, bf16[6,345,4,64]{1,3,2,0:T(8,128)(2,1)}, s32[6,345]{1,0:...) while((s32[]{:T(128)}, ...), condition=%wide.region_6.7_spmd, body=%wide.region_3.6_spmd.sunk | while | flops 127800768 | bytes 7319127 | solution.py:173
  118.2 6.1 fusion.89
  126.0 9.5 collective-permute-done
  135.6 4.7 collective-permute-start.4
  140.3 5.2 collective-permute-done.1
  150.2 7.5 collective-permute-done.2
  162.7 7.3 collective-permute-done.3
  179.6 3.6 gather_fusion
  183.2 10.9 %fusion.90 = f32[2070,1024]{1,0:T(8,128)} fusion(bf16[2070,1024]{1,0:T(8,128)(2,1)} %param.33, bf16[1024,1024]{1,0:T(8,128)(2,1)} %all-gather.5.cloned.1.call-done), kind=kOutput, calls=%fused_computation.159 | convolution fusion | flops 4341104640 | bytes 14815232 | tf_op jit(solution)/shard_map/td,fd->tf/dot_general | solution.py:188
  194.0 84.5 %all-reduce.7.cloned.1.call-done = f32[2070,1024]{1,0:T(8,128)} async-done(((f32[2070,1024]{1,0:T(8,128)}), f32[2070,1024]{1,0:T(8,128)}) %all-reduce.7.cloned.1.call-update) | async-done | bytes 8478736 | tf_op jit(solution)/shard_map/psum | solution.py:178
  278.6 5.8 fusion.84
  288.0 14.3 %fusion.82 = (f32[1024]{0:T(1024)}, bf16[2070,1024]{1,0:T(8,128)(2,1)S(1)}, bf16[2070,1024]{1,0:T(8,128)(2,1)}) fusion(f32[2070,1024]{1,0:T(8,128)} %fusion.90, f32[1024]{0:T(1024)S(1)} %copy-done.33, bf16[1024,1024]{1,0:T(8,128)(2,1)S(1)} %bitcast.161, f32[2070,1024]{1,0:T(8,128)S(1)} %get-tuple-element.241, f32[1024]{0:T(1024)S(1)} %copy-done.34, ...), kind=kOutput, calls=%fused_computation.152 | convolution fusion | flops 4387736576 | bytes 27566256 | tf_op jit(solution)/shard_map/dot_general | solution.py:41
  304.3 7.1 fusion.65
  311.7 9.2 convolution_convert_fusion.3
  320.9 4.0 copy.119
  325.0 12.1 %fusion.67 = bf16[1024,1024]{1,0:T(8,128)(2,1)} fusion(bf16[2070,1024]{1,0:T(8,128)(2,1)} %copy-done.37, f32[2070,1024]{1,0:T(8,128)} %copy-done, f32[1024]{0:T(1024)S(1)} %copy-done.34, f32[1024]{0:T(1024)S(1)} %copy-done.25, f32[2070]{0:T(1024)S(1)} %fusion.79, f32[2070]{0:T(1024)S(1)} %broadcast_multiply_fusion), kind=kOutput, calls=%fused_computation.111 | convolution fusion | flops 4352751616 | bytes 14839984 | tf_op jit(solution)/shard_map/td,tf->df/dot_general | solution.py:195
  337.6 128.8 %all-reduce.9.cloned.1.call-done = f32[2070,1024]{1,0:T(8,128)} async-done(((f32[2070,1024]{1,0:T(8,128)}), f32[2070,1024]{1,0:T(8,128)}) %all-reduce.9.cloned.1.call-update) | async-done | bytes 8478736 | tf_op jit(solution)/shard_map/psum | solution.py:201
  466.4 8.2 multiply_reduce_fusion.1
  474.7 5.7 fusion.83
  480.4 3.4 copy-done.2
  487.8 4.0 copy.100
  491.8 45.9 %while.27 = (s32[]{:T(128)}, f32[6,345,4,64]{1,3,2,0:T(8,128)}, bf16[6,345,4,64]{1,3,2,0:T(8,128)(2,1)}, f32[6,345,4,64]{1,3,2,0:T(8,128)}, bf16[6,345,4,64]{1,3...) while((s32[]{:T(128)}, f32[6,345,4,64]{1,3,2,0:T(8,128)}, ...), condition=%wide.region_16.17_spmd, body=%wide.region_14.16_spmd.sunk | while | flops 309283200 | bytes 17905560 | solution.py:216
  537.7 7.1 fusion.70
  545.8 5.6 fusion.87
  551.4 4.0 copy.114
  557.9 3.9 copy.115
  573.2 9.4 convolution_convert_fusion.4
  582.6 9.6 convolution_convert_fusion.1
  592.2 5.1 bitcast_convert_fusion
  599.3 8.7 reduce-scatter.11.cloned.1.call-done
  610.0 20.2 %all-reduce.1 = (f32[2,256]{1,0:T(2,128)}, f32[1024]{0:T(1024)}) all-reduce(f32[2,256]{1,0:T(2,128)S(1)} %pad_maximum_fusion, f32[1024]{0:T(1024)S(1)} %copy-done.28), channel_id=1, replica_groups=mesh['dp'=8,'mp'=4] {'dp'}, use_global_device_ids=true, to_apply=%region_27.28 | all-reduce | flops 1536 | bytes 12288 | tf_op jit(solution)/shard_map/psum | solution.py:251
  630.2 42.0 %reduce-scatter.13.cloned.1.call-done = bf16[128,256]{1,0:T(8,128)(2,1)} async-done(((bf16[1024,256]{1,0:T(8,128)(2,1)}), bf16[128,256]{1,0:T(8,128)(2,1)}) %reduce-scatter.13.cloned.1.call-update) | async-done | bytes 65552
  673.9 66.7 %reduce-scatter.9.cloned.1.call-done = bf16[128,3,256]{2,0,1:T(8,128)(2,1)} async-done(((bf16[1024,3,256]{2,0,1:T(8,128)(2,1)}), bf16[128,3,256]{2,0,1:T(8,128)(2,1)}) %reduce-scatter.9.cloned.1.call-update) | async-done | bytes 196624 | tf_op jit(solution)/shard_map/reduce_scatter | solution.py:238
  742.3 155.7 %all-reduce.11.cloned.1.call-done = (bf16[2070,1024]{1,0:T(8,128)(2,1)}, bf16[2070,1024]{1,0:T(8,128)(2,1)}) async-done(((bf16[2070,1024]{1,0:T(8,128)(2,1)}, bf16[2070,1024]{1,0:T(8,128)(2,1)}), (bf16[2070,1024]{1,0:T(8,128)(2,1)}, bf16[2070,1024]{1,0:T(8,128)(2,1)})) %all-reduce.11.cloned.1.call-update) | async-done | bytes 8478736 | tf_op jit(solution)/shard_map/psum | solution.py:184
  898.0 5.4 fusion.56
  903.4 14.0 %fusion.54 = (f32[1024]{0:T(1024)S(1)}, f32[1024]{0:T(1024)S(1)}, f32[1024]{0:T(1024)S(1)}, f32[2070]{0:T(1024)S(1)}, f32[1024]{0:T(1024)S(1)}) fusion(bf16[2070,1024]{1,0:T(8,128)(2,1)} %param.33, f32[2070]{0:T(1024)S(1)} %copy-done.19, f32[2070,1024]{1,0:T(8,128)} %copy-done.2, f32[2070]{0:T(1024)S(1)} %negate_multiply_fusion.1, ...), kind=kLoop, calls=%fused_computation.80 | loop fusion | flops 44507112 | bytes 21266960 | tf_op jit(solution)/shard_map/reduce_sum | solution.py:208
  917.4 13.7 %add_add_fusion.2 = f32[2070,1024]{1,0:T(8,128)} fusion(bf16[2070,1024]{1,0:T(8,128)(2,1)} %param.19, bf16[2070,1024]{1,0:T(8,128)(2,1)} %get-tuple-element.235, f32[2070]{0:T(1024)S(1)} %negate_multiply_fusion, f32[2070]{0:T(1024)S(1)} %multiply_multiply_fusion, f32[1024]{0:T(1024)S(1)} %copy-done.24, f32[2070]{0:T(1024)S(1)} %copy-done.17, ...), kind=kLoop, calls=%fused_computation.87 | loop fusion | flops 27555840 | bytes 29721016 | tf_op jit(solution)/shard_map/add | solution.py:233
  931.2 7.1 add_convert_fusion
  938.3 39.9 %all-reduce = (f32[1024]{0:T(1024)}, f32[1024]{0:T(1024)}, f32[1024]{0:T(1024)}, f32[1024]{0:T(1024)}, f32[1024]{0:T(1024)}, /*index=5*/f32[1024]{0:T(1024)}) all-reduce(f32[1024]{0:T(1024)S(1)} %get-tuple-element.189, f32[1024]{0:T(1024)S(1)} %get-tuple-element.187, ...), channel_id=1, replica_groups=mesh['dp'=8,'mp'=4] {'dp','mp'}, use_global_device_ids=true, to_apply=%region_21.22 | all-reduce | flops 6144 | bytes 49152 | tf_op jit(solution)/shard_map/psum | solution.py:252
  (267 shorter events, 138.7 us)
Async XLA Ops:
  7.2 53.6 %all-gather.3.cloned.1.call-start = ((), (), s32[]{:S(2)}) async-start(), calls=%async_computation.4 | async-start | bytes 1769472 | tf_op jit(solution)/shard_map/all_gather | solution.py:161
  8.9 174.2 %all-gather.5.cloned.1.call-start = ((), (), s32[]{:S(2)}) async-start(), calls=%async_computation.6 | async-start | bytes 2359296 | tf_op jit(solution)/shard_map/all_gather | solution.py:164
  10.8 267.8 %all-reduce.7.cloned.1.call-start = ((), (), s32[]{:S(2)}) async-start(), calls=%async_computation.5 | async-start | bytes 16973824 | tf_op jit(solution)/shard_map/psum | solution.py:178
  10.9 5.4 copy-start.31
  10.9 5.6 copy-start.29
  10.9 5.7 copy-start.15
  10.9 49.9 %copy-start.23 = (f32[1024]{0:T(1024)S(1)}, f32[1024]{0:T(1024)}, u32[]{:S(2)}) copy-start(f32[1024]{0:T(1024)} %param.21) | copy-start | bytes 12292
  10.9 49.9 %copy-start.35 = (f32[1024]{0:T(1024)S(1)}, f32[1024]{0:T(1024)}, u32[]{:S(2)}) copy-start(f32[1024]{0:T(1024)} %param.22) | copy-start | bytes 12292
  14.3 46.4 %copy-start.12 = (f32[2070]{0:T(1024)}, f32[2070]{0:T(1024)S(1)}, u32[]{:S(2)}) copy-start(f32[2070]{0:T(1024)S(1)} %broadcast_multiply_fusion.1) | copy-start | bytes 24844
  16.2 44.5 %copy-start.16 = (f32[2070]{0:T(1024)}, f32[2070]{0:T(1024)S(1)}, u32[]{:S(2)}) copy-start(f32[2070]{0:T(1024)S(1)} %fusion.78) | copy-start | bytes 24844
  82.9 8.8 copy-start.10
  113.5 10.8 %copy-start.22 = (s32[6,345]{1,0:T(8,128)}, s32[6,345]{1,0:T(8,128)S(1)}, u32[]{:S(2)}) copy-start(s32[6,345]{1,0:T(8,128)S(1)} %get-tuple-element.479) | copy-start | bytes 24844
  118.1 6.2 copy-start.4
  124.3 342.1 %all-reduce.9.cloned.1.call-start = ((), (), s32[]{:S(2)}) async-start(), calls=%async_computation.7 | async-start | bytes 16973824 | tf_op jit(solution)/shard_map/psum | solution.py:201
  125.4 10.2 %collective-permute-start = (bf16[128,1024]{1,0:T(8,128)(2,1)S(1)}, bf16[128,1024]{1,0:T(8,128)(2,1)S(1)}, u32[]{:S(2)}, u32[]{:S(2)}) collective-permute-start(bf16[128,1024]{1,0:T(8,128)(2,1)S(1)} %convert_element_type.123), channel_id=1, source_target_pairs={{0,4},{4,8},{8,12},{12,16},{16,20},{20,24},{24,28},{28,0},{1,5},{5... | collective-permute-start | bytes 786440 | tf_op jit(solution)/shard_map/ppermute | solution.py:126
  135.6 9.9 %collective-permute-start.1 = (bf16[128,1024]{1,0:T(8,128)(2,1)S(1)}, bf16[128,1024]{1,0:T(8,128)(2,1)S(1)}, u32[]{:S(2)}, u32[]{:S(2)}) collective-permute-start(bf16[128,1024]{1,0:T(8,128)(2,1)S(1)} %collective-permute-done), channel_id=1, source_target_pairs={{0,4},{4,8},{8,12},{12,16},{16,20},{20,24},{24,28},{28,0},{1,5},{5... | collective-permute-start | bytes 786440 | tf_op jit(solution)/shard_map/ppermute | solution.py:126
  135.6 12.4 %collective-permute-start.4 = (bf16[128,1024]{1,0:T(8,128)(2,1)S(1)}, bf16[128,1024]{1,0:T(8,128)(2,1)S(1)}, u32[]{:S(2)}, u32[]{:S(2)}) collective-permute-start(bf16[128,1024]{1,0:T(8,128)(2,1)S(1)} %convert_element_type.123), channel_id=1, source_target_pairs={{4,0},{8,4},{12,8},{16,12},{20,16},{24,20},{28,24},{0,28},{5,1},{9... | collective-permute-start | bytes 786440 | tf_op jit(solution)/shard_map/ppermute | solution.py:132
  145.5 12.2 %collective-permute-start.2 = (bf16[128,1024]{1,0:T(8,128)(2,1)S(1)}, bf16[128,1024]{1,0:T(8,128)(2,1)}, u32[]{:S(2)}, u32[]{:S(2)}) collective-permute-start(bf16[128,1024]{1,0:T(8,128)(2,1)S(1)} %collective-permute-done.1), channel_id=1, source_target_pairs={{0,4},{4,8},{8,12},{12,16},{16,20},{20,24},{24,28},{28,0},{1,5},{5... | collective-permute-start | bytes 786440 | tf_op jit(solution)/shard_map/ppermute | solution.py:126
  148.0 12.4 %collective-permute-start.5 = (bf16[128,1024]{1,0:T(8,128)(2,1)S(1)}, bf16[128,1024]{1,0:T(8,128)(2,1)}, u32[]{:S(2)}, u32[]{:S(2)}) collective-permute-start(bf16[128,1024]{1,0:T(8,128)(2,1)S(1)} %collective-permute-done.4), channel_id=1, source_target_pairs={{4,0},{8,4},{12,8},{16,12},{20,16},{24,20},{28,24},{0,28},{5,1},{9... | collective-permute-start | bytes 786440 | tf_op jit(solution)/shard_map/ppermute | solution.py:132
  157.7 12.3 %collective-permute-start.3 = (bf16[128,1024]{1,0:T(8,128)(2,1)}, bf16[128,1024]{1,0:T(8,128)(2,1)}, u32[]{:S(2)}, u32[]{:S(2)}) collective-permute-start(bf16[128,1024]{1,0:T(8,128)(2,1)} %collective-permute-done.2), channel_id=1, source_target_pairs={{0,4},{4,8},{8,12},{12,16},{16,20},{20,24},{24,28},{28,0},{1,5},{5... | collective-permute-start | bytes 786440 | tf_op jit(solution)/shard_map/ppermute | solution.py:126
  160.3 18.5 %collective-permute-start.6 = (bf16[128,1024]{1,0:T(8,128)(2,1)}, bf16[128,1024]{1,0:T(8,128)(2,1)S(1)}, u32[]{:S(2)}, u32[]{:S(2)}) collective-permute-start(bf16[128,1024]{1,0:T(8,128)(2,1)} %collective-permute-done.5), channel_id=1, source_target_pairs={{4,0},{8,4},{12,8},{16,12},{20,16},{24,20},{28,24},{0,28},{5,1},{9... | collective-permute-start | bytes 786440 | tf_op jit(solution)/shard_map/ppermute | solution.py:132
  183.2 95.4 %copy-start.30 = (f32[1024]{0:T(1024)S(1)}, f32[1024]{0:T(1024)}, u32[]{:S(2)}) copy-start(f32[1024]{0:T(1024)} %param.26) | copy-start | bytes 12292
  284.4 3.6 copy-start
  284.4 3.6 copy-start.9
  311.4 285.9 %reduce-scatter.15.cloned.1.call-start = ((), (), s32[]{:S(2)}) async-start(), calls=%async_computation.11 | async-start | bytes 2359296
  324.8 283.2 %reduce-scatter.11.cloned.1.call-start = ((), (), s32[]{:S(2)}) async-start(), calls=%async_computation.9 | async-start | bytes 2359296 | tf_op jit(solution)/shard_map/reduce_scatter | solution.py:244
  324.9 141.5 %copy-start.18 = (f32[2070]{0:T(1024)}, f32[2070]{0:T(1024)S(1)}, u32[]{:S(2)}) copy-start(f32[2070]{0:T(1024)S(1)} %fusion.77) | copy-start | bytes 24844
  337.1 335.2 %reduce-scatter.13.cloned.1.call-start = ((), (), s32[]{:S(2)}) async-start(), calls=%async_computation.10 | async-start | bytes 589824
  466.4 8.3 copy-start.3
  466.4 17.4 %slice-start = ((s8[4243456]{0:T(1024)(128)(4,1)}), s8[4194304]{0:T(1024)(128)(4,1)S(1)}, s32[]{:S(2)}) async-start(s8[4243456]{0:T(1024)(128)(4,1)} %bitcast.156), calls=%async_computation.13 | async-start | bytes 8388608
  474.7 9.1 slice-start.1
  474.7 9.1 copy-start.7
  566.0 5.1 copy-start.5
  566.0 7.2 copy-start.13
  566.0 7.2 copy-start.17
  566.0 7.2 copy-start.24
  566.0 7.2 copy-start.36
  571.0 169.6 %reduce-scatter.9.cloned.1.call-start = ((), (), s32[]{:S(2)}) async-start(), calls=%async_computation.8 | async-start | bytes 1769472 | tf_op jit(solution)/shard_map/reduce_scatter | solution.py:238
  582.6 9.7 copy-start.11
  582.6 315.4 %all-reduce.11.cloned.1.call-start = ((), (), s32[]{:S(2)}) async-start(), calls=%async_computation.12 | async-start | bytes 16973824 | tf_op jit(solution)/shard_map/psum | solution.py:184
  582.6 9.6 copy-start.32
  597.3 12.7 %copy-start.28 = (f32[1024]{0:T(1024)S(1)}, f32[1024]{0:T(1024)}, u32[]{:S(2)}) copy-start(f32[1024]{0:T(1024)} %get-tuple-element.236) | copy-start | bytes 12292
  898.0 5.4 copy-start.21
  898.0 5.4 copy-start.19
  903.4 27.7 %slice-start.2 = ((s8[4243456]{0:T(1024)(128)(4,1)}), s8[49152]{0:T(1024)(128)(4,1)S(1)}, s32[]{:S(2)}) async-start(s8[4243456]{0:T(1024)(128)(4,1)} %bitcast.159), calls=%async_computation.15 | async-start | bytes 98304
  917.4 13.7 %slice-start.3 = ((s8[4243456]{0:T(1024)(128)(4,1)}), s8[4194304]{0:T(1024)(128)(4,1)S(1)}, s32[]{:S(2)}) async-start(s8[4243456]{0:T(1024)(128)(4,1)} %bitcast.159), calls=%async_computation.16 | async-start | bytes 8388608
  917.4 13.7 %copy-start.27 = (f32[1024]{0:T(1024)S(1)}, f32[1024]{0:T(1024)}, u32[]{:S(2)}) copy-start(f32[1024]{0:T(1024)} %param.32) | copy-start | bytes 12292
  931.2 7.1 copy-start.26
  (10 other events, 27.4 us)
Sparse Core Ops, SparseCore 0:
  10.8 49.9 all-gather.2
  63.4 50.3 all-gather.4
  124.5 154.0 all-reduce.6
  311.6 154.8 all-reduce.8
  469.8 67.8 reduce-scatter.14
  541.1 66.8 reduce-scatter.10
  611.4 60.8 reduce-scatter.12
  676.1 64.4 reduce-scatter.8
  743.8 154.1 all-reduce.10
